TPU v7x, 256 devices: a whole 4x4x8 slice. The times are simulated.
256 devices in a mesh: frame: 16 (over z_hi, y, core), row: 16 (over x, z_lo).
Axes of the slice: x: 4, y: 4, z: 8 (z_hi: 2, z_lo: 4; z = z_hi * 4 + z_lo), core: 2. Of those that a mesh axis runs over, the one named last changes fastest.
Arguments:
- latent: bfloat16 [64, 32, 240, 320], P('frame', 'row'), may hold values from -6 to 6
- gain_one: float32 [320], replicated, may hold values from 0.1 to 1.9
- spatial_weight: bfloat16 [3, 3, 320, 320], replicated, may hold values from -0.109375 to 0.109375
- gain_two: float32 [320], replicated, may hold values from 0.1 to 1.9
- temporal_weight: bfloat16 [3, 320, 320], replicated, may hold values from -0.1875 to 0.1875
- gain_three: float32 [320], replicated, may hold values from 0.1 to 1.9
- query_weight: bfloat16 [320, 320], replicated, as said below
- key_weight: bfloat16 [320, 320], replicated, may hold values from -0.3125 to 0.3125
- value_weight: bfloat16 [320, 320], replicated, may hold values from -0.3125 to 0.3125
- out_weight: bfloat16 [320, 320], replicated, may hold values from -0.3125 to 0.3125
Outputs:
- block_out: float32 [64, 32, 240, 320], P('frame', 'row')
Inputs may be any that keep to these rules, and one draw needn't show every extreme that they name: `query_weight`: a projection matrix.
All inputs are finite; a program needn't handle non-finite values.
Results may differ from a plain program's by a relative error of at most 0.012.
The roundings to bfloat16 on the way count: a program that leaves them out, or rounds other values in their place, can miss the bound.
Values may be sent and summed in bfloat16 or wider, within the bound.
A program may use at most 128 MiB of HBM per device.

v0:
```python
import jax
import jax.numpy as jnp
from jax import lax
from jax.sharding import PartitionSpec as P

HEAD_DIM = 64


def extended(cells, sides, width):
    for axis, dim in sides:
        count = lax.axis_size(axis)
        ends = count - 1
        head = lax.slice_in_dim(cells, 0, width, axis=dim)
        tail = lax.slice_in_dim(cells, cells.shape[dim] - width, cells.shape[dim], axis=dim)
        cells = jnp.concatenate(
            [
                lax.ppermute(tail, axis, [(i, (i + 1) % count) for i in range(ends)]),
                cells,
                lax.ppermute(head, axis, [((i + 1) % count, i) for i in range(ends)]),
            ],
            axis=dim,
        )
    return cells


def rms_norm(values, gain):
    mean_sq = jnp.mean(values * values, axis=-1, keepdims=True)
    return values * lax.rsqrt(mean_sq + 1e-06) * gain


def project(normed, weight):
    chans = normed.shape[-1]
    flat = jnp.dot(normed.reshape(-1, chans), weight, preferred_element_type=jnp.float32)
    return flat.astype(jnp.bfloat16).reshape(normed.shape[:-1] + (weight.shape[1],))


def attend_heads(queries, keys, values):
    frames, pixels, chans = queries.shape
    heads = chans // HEAD_DIM
    q_split = queries.reshape(frames, pixels, heads, HEAD_DIM)
    k_split = keys.reshape(frames, pixels, heads, HEAD_DIM)
    v_split = values.reshape(frames, pixels, heads, HEAD_DIM)
    scores = jnp.einsum(
        "fphd,gphd->phfg", q_split, k_split, preferred_element_type=jnp.float32
    ) / jnp.sqrt(jnp.float32(HEAD_DIM))
    peak = jnp.max(scores, axis=-1, keepdims=True)
    expo = jnp.exp(scores - peak)
    total = jnp.sum(expo, axis=-1)
    weight = expo.astype(jnp.bfloat16)
    summed = jnp.einsum("phfg,gphd->fphd", weight, v_split, preferred_element_type=jnp.float32)
    summed = summed / jnp.transpose(total, (2, 0, 1))[..., None]
    return summed.reshape(frames, pixels, chans).astype(jnp.bfloat16)


def temporal_mix(padded, temporal_weight, frames):
    chans = padded.shape[-1]
    pixels = padded.shape[1]
    total = jnp.zeros((frames * pixels, chans), jnp.float32)
    for tap in range(3):
        total = total + jnp.dot(
            padded[tap : tap + frames].reshape(-1, chans),
            temporal_weight[tap],
            preferred_element_type=jnp.float32,
        )
    return total.reshape(frames, pixels, chans)


def local(
    latent,
    gain_one,
    spatial_weight,
    gain_two,
    temporal_weight,
    gain_three,
    query_weight,
    key_weight,
    value_weight,
    out_weight,
):
    frames_here, rows_here, width, chans = latent.shape
    source = latent.astype(jnp.float32)
    act_one = jax.nn.silu(rms_norm(source, gain_one)).astype(jnp.bfloat16)
    rimmed = extended(act_one, (("row", 1),), 1)
    spatial = lax.conv_general_dilated(
        rimmed,
        spatial_weight,
        (1, 1),
        ((0, 0), (1, 1)),
        dimension_numbers=("NHWC", "HWIO", "NHWC"),
        preferred_element_type=jnp.float32,
    )
    hidden_one = source + spatial
    pixels = rows_here * width
    hidden_flat = hidden_one.reshape(frames_here, pixels, chans)
    act_two = jax.nn.silu(rms_norm(hidden_flat, gain_two)).astype(jnp.bfloat16)
    padded = extended(act_two, (("frame", 0),), 1)
    temporal = temporal_mix(padded, temporal_weight, frames_here)
    hidden_two = hidden_flat + temporal
    normed = rms_norm(hidden_two, gain_three).astype(jnp.bfloat16)
    groups = lax.axis_size("frame")
    per_group = pixels // groups
    moved = lax.all_to_all(
        normed.reshape(frames_here, groups, per_group, chans),
        "frame",
        split_axis=1,
        concat_axis=0,
        tiled=True,
    )
    moved = moved.reshape(frames_here * groups, per_group, chans)
    attended = attend_heads(
        project(moved, query_weight), project(moved, key_weight), project(moved, value_weight)
    ).reshape(frames_here * groups, 1, per_group, chans)
    returned = lax.all_to_all(attended, "frame", split_axis=0, concat_axis=1, tiled=True)
    mixed = jnp.dot(returned.reshape(-1, chans), out_weight, preferred_element_type=jnp.float32)
    result = hidden_two.reshape(-1, chans) + mixed
    return result.reshape(frames_here, rows_here, width, chans)


def solution(mesh):
    return jax.shard_map(
        local,
        mesh=mesh,
        in_specs=(P("frame", "row", None, None), P(), P(), P(), P(), P(), P(), P(), P(), P()),
        out_specs=P("frame", "row", None, None),
        check_vma=False,
    )
```

profile of v0, /device:TPU:63, one launch (start us, length us, event | category | flops | bytes accessed | tf_op | source)
XLA Modules:
  0.0 391.0 jit_solution(15593227416273346015)
XLA Ops:
  17.7 11.6 %collective-permute-done.1 = bf16[4,1,240,320]{2,3,1,0:T(8,128)(2,1)} collective-permute-done((bf16[4,1,240,320]{2,3,1,0:T(8,128)(2,1)}, bf16[4,1,240,320]{2,3,1,0:T(8,128)(2,1)}, u32[]{:S(2)}, u32[]{:S(2)}) %collective-permute-start.1) | collective-permute-done | bytes 614432 | tf_op jit(solution)/shard_map/ppermute | solution.py:19
  30.8 15.3 %collective-permute-done = bf16[4,1,240,320]{2,3,1,0:T(8,128)(2,1)} collective-permute-done((bf16[4,1,240,320]{2,3,1,0:T(8,128)(2,1)}, bf16[4,1,240,320]{2,3,1,0:T(8,128)(2,1)}, u32[]{:S(2)}, u32[]{:S(2)}) %collective-permute-start) | collective-permute-done | bytes 614432 | tf_op jit(solution)/shard_map/ppermute | solution.py:17
  53.4 5.8 %reshape.119 = bf16[4,4,8,31,320]{4,3,2,1,0:T(8,128)(2,1)} reshape(bf16[4,4,248,320]{3,2,1,0:T(8,128)(2,1)} %pad) | data formatting | bytes 5079040 | tf_op jit(solution)/shard_map/conv_general_dilated | solution.py:84
  62.8 6.6 %fusion.25 = f32[2,32,31,320]{3,1,2,0:T(8,128)S(1)} fusion(bf16[3,3,320,320]{3,2,1,0:T(8,128)(2,1)S(1)} %copy-done, bf16[4,4,8,33,320]{4,3,2,1,0:T(8,128)(2,1)S(1)} %fusion.4, pred[32,31]{0,1:T(8,128)(4,1)S(1)} %copy-done.15), kind=kOutput, calls=%fused_computation.42 | convolution fusion | flops 3657543680 | bytes 7087072 | tf_op jit(solution)/shard_map/conv_general_dilated | solution.py:84
  88.1 4.9 %copy.81 = bf16[4,2,240,320]{2,1,0,3:T(2,128)(2,1)} copy(bf16[4,2,240,320]{3,2,0,1:T(8,128)(2,1)} %multiply_convert_fusion) | data formatting | bytes 2457600 | tf_op jit(solution)/shard_map/convert_element_type | solution.py:95
  93.0 4.9 %convert_element_type.48 = bf16[1920,320]{0,1:T(8,128)(2,1)} reshape(bf16[4,2,240,320]{2,1,0,3:T(2,128)(2,1)} %copy.81) | data formatting | bytes 2457600 | tf_op jit(solution)/shard_map/convert_element_type | solution.py:95
  97.9 4.8 %reshape.109 = f32[4,480,320]{1,2,0:T(8,128)} reshape(f32[4,2,240,320]{2,1,3,0:T(2,128)} %copy.78) | data formatting | bytes 4915200 | tf_op jit(solution)/shard_map/reshape | solution.py:94
  108.9 8.1 %collective-permute-start.2 = (bf16[1,480,320]{1,2,0:T(8,128)(2,1)S(1)}, bf16[1,480,320]{1,2,0:T(8,128)(2,1)S(1)}, u32[]{:S(2)}, u32[]{:S(2)}) collective-permute-start(bf16[1,480,320]{1,2,0:T(8,128)(2,1)S(1)} %get-tuple-element.12), channel_id=1, source_target_pairs={{0,16},{16,32},{32,48},{48,64},{64,80},{80,96},{96,112},{112,128},... | collective-permute-start | bytes 921608 | tf_op jit(solution)/shard_map/ppermute | solution.py:17
  146.2 6.7 %reshape.114 = f32[4,2,240,320]{2,1,0,3:T(2,128)} reshape(f32[1920,320]{0,1:T(8,128)} %convolution_add_fusion.1) | data formatting | bytes 4915200 | tf_op jit(solution)/shard_map/reshape | solution.py:65
  156.3 5.6 %copy.86 = f32[4,2,240,320]{3,2,0,1:T(8,128)} copy(f32[4,2,240,320]{2,1,0,3:T(2,128)} %reshape.114) | data formatting | bytes 4915200 | tf_op jit(solution)/shard_map/reshape | solution.py:65
  168.5 5.0 %fusion.18 = bf16[4,16,30,320]{3,0,2,1:T(4,128)(2,1)S(1)} fusion(f32[4,16,30,320]{3,0,2,1:T(4,128)} %bitcast.76, f32[4,16,30,320]{3,2,1,0:T(8,128)} %reshape.113, f32[320]{0:T(512)S(1)} %copy-done.14, f32[4,16,30]{0,2,1:T(8,128)S(1)} %copy.88), kind=kLoop, calls=%fused_computation.28 | loop fusion | flops 2457600 | bytes 6152960 | tf_op jit(solution)/shard_map/convert_element_type | solution.py:99
  173.5 48.7 %all_to_all.30 = bf16[4,16,30,320]{3,0,2,1:T(4,128)(2,1)S(1)} all-to-all(bf16[4,16,30,320]{3,0,2,1:T(4,128)(2,1)S(1)} %fusion.18), channel_id=1, replica_groups=mesh['frame'=16,'row'=16] {'frame'}, dimensions={1} | all-to-all | bytes 2457600 | tf_op jit(solution)/shard_map/all_to_all | solution.py:102
  234.6 15.4 %reshape.127 = bf16[64,30,5,64]{1,0,3,2:T(8,128)(2,1)} reshape(bf16[1920,320]{0,1:T(8,128)(2,1)} %convolution_convert_fusion.2) | data formatting | bytes 2457600 | tf_op jit(solution)/shard_map/reshape;reshape | solution.py:42
  250.0 7.3 %copy.95 = bf16[64,30,5,64]{0,3,2,1:T(8,128)(2,1)} copy(bf16[64,30,5,64]{1,0,3,2:T(8,128)(2,1)} %reshape.127) | data formatting | bytes 2457600 | tf_op jit(solution)/shard_map/reshape;reshape | solution.py:42
  257.3 15.4 %reshape.128 = bf16[64,30,5,64]{1,0,3,2:T(8,128)(2,1)} reshape(bf16[1920,320]{0,1:T(8,128)(2,1)} %convolution_convert_fusion.1) | data formatting | bytes 2457600 | tf_op jit(solution)/shard_map/reshape;reshape | solution.py:40
  272.7 9.9 %copy.93 = bf16[64,30,5,64]{3,0,2,1:T(8,128)(2,1)} copy(bf16[64,30,5,64]{1,0,3,2:T(8,128)(2,1)} %reshape.128) | data formatting | bytes 2457600 | tf_op jit(solution)/shard_map/reshape;reshape | solution.py:40
  282.6 15.6 %reshape.129 = bf16[64,30,5,64]{1,0,3,2:T(8,128)(2,1)} reshape(bf16[1920,320]{0,1:T(8,128)(2,1)} %convolution_convert_fusion) | data formatting | bytes 2457600 | tf_op jit(solution)/shard_map/reshape;reshape | solution.py:41
  298.2 10.0 %copy.94 = bf16[64,30,5,64]{3,0,2,1:T(8,128)(2,1)} copy(bf16[64,30,5,64]{1,0,3,2:T(8,128)(2,1)} %reshape.129) | data formatting | bytes 2457600 | tf_op jit(solution)/shard_map/reshape;reshape | solution.py:41
  316.5 4.7 %copy.97 = bf16[64,1,30,320]{3,2,1,0:T(8,128)(2,1)} copy(bf16[64,1,30,320]{0,3,2,1:T(8,128)(2,1)} %bitcast.79) | data formatting | bytes 2457600 | tf_op jit(solution)/shard_map/convert_element_type | solution.py:52
  321.2 6.4 %all-to-all-start.1 = ((bf16[64,1,30,320]{3,2,1,0:T(8,128)(2,1)}), bf16[64,1,30,320]{3,2,1,0:T(8,128)(2,1)}, u32[]{:S(2)}, u32[]{:S(2)}) async-start(bf16[64,1,30,320]{3,2,1,0:T(8,128)(2,1)} %copy.97), calls=%async_computation.1 | async-start | bytes 3145728 | tf_op jit(solution)/shard_map/all_to_all | solution.py:113
  330.9 5.0 %reshape.108 = f32[1920,320]{0,1:T(8,128)} reshape(f32[4,2,240,320]{2,1,0,3:T(2,128)} %copy.77) | data formatting | bytes 4915200 | tf_op jit(solution)/shard_map/reshape | solution.py:94
  335.9 31.6 %all-to-all-done.1 = bf16[64,1,30,320]{3,2,1,0:T(8,128)(2,1)} async-done(((bf16[64,1,30,320]{3,2,1,0:T(8,128)(2,1)}), bf16[64,1,30,320]{3,2,1,0:T(8,128)(2,1)}, u32[]{:S(2)}, u32[]{:S(2)}) %all-to-all-start.1) | async-done | bytes 1228832 | tf_op jit(solution)/shard_map/all_to_all | solution.py:113
  375.3 4.5 %convolution_add_fusion = f32[1920,320]{0,1:T(8,128)} fusion(bf16[1920,320]{1,0:T(8,128)(2,1)} %reshape.115, bf16[320,320]{1,0:T(8,128)(2,1)S(1)} %copy-done.11, f32[1920,320]{0,1:T(8,128)} %reshape.108, f32[1920,320]{0,1:T(8,128)S(1)} %copy-done.2), kind=kOutput, calls=%fused_computation.32 | convolution fusion | flops 394444800 | bytes 8806400 | tf_op jit(solution)/shard_map/dot_general | solution.py:114
  379.8 6.9 %reshape.116 = f32[4,2,240,320]{2,1,0,3:T(2,128)} reshape(f32[1920,320]{0,1:T(8,128)} %convolution_add_fusion) | data formatting | bytes 4915200 | tf_op jit(solution)/shard_map/reshape | solution.py:116
  (89 shorter events, 129.7 us)
Async XLA Ops:
  0.0 62.8 %copy-start = (bf16[3,3,320,320]{3,2,1,0:T(8,128)(2,1)S(1)}, bf16[3,3,320,320]{3,2,1,0:T(8,128)(2,1)}, u32[]{:S(2)}) copy-start(bf16[3,3,320,320]{3,2,1,0:T(8,128)(2,1)} %param.12) | copy-start | bytes 5529604
  0.0 4.5 %copy-start.13 = (f32[320]{0:T(512)S(1)}, f32[320]{0:T(512)}, u32[]{:S(2)}) copy-start(f32[320]{0:T(512)} %param.11) | copy-start | bytes 3844
  6.8 1.1 copy-start.4
  11.2 18.2 %collective-permute-start.1 = (bf16[4,1,240,320]{2,3,1,0:T(8,128)(2,1)}, bf16[4,1,240,320]{2,3,1,0:T(8,128)(2,1)}, u32[]{:S(2)}, u32[]{:S(2)}) collective-permute-start(bf16[4,1,240,320]{2,3,1,0:T(8,128)(2,1)} %copy.72), channel_id=1, source_target_pairs={{1,0},{2,1},{3,2},{4,3},{5,4},{6,5},{7,6},{8,7},{9,8},{10,9},{11,1... | collective-permute-start | bytes 1843208 | tf_op jit(solution)/shard_map/ppermute | solution.py:19
  14.2 31.9 %collective-permute-start = (bf16[4,1,240,320]{2,3,1,0:T(8,128)(2,1)}, bf16[4,1,240,320]{2,3,1,0:T(8,128)(2,1)}, u32[]{:S(2)}, u32[]{:S(2)}) collective-permute-start(bf16[4,1,240,320]{2,3,1,0:T(8,128)(2,1)} %copy.71), channel_id=1, source_target_pairs={{0,1},{1,2},{2,3},{3,4},{4,5},{5,6},{6,7},{7,8},{8,9},{9,10},{10,1... | collective-permute-start | bytes 1843208 | tf_op jit(solution)/shard_map/ppermute | solution.py:17
  60.4 2.4 copy-start.15
  83.2 2.9 copy-start.12
  102.7 14.4 %copy-start.5 = (bf16[1920,320]{0,1:T(8,128)(2,1)S(1)}, bf16[1920,320]{0,1:T(8,128)(2,1)}, u32[]{:S(2)}) copy-start(bf16[1920,320]{0,1:T(8,128)(2,1)} %convert_element_type.48) | copy-start | bytes 3686404
  105.5 17.9 %collective-permute-start.3 = (bf16[1,480,320]{1,2,0:T(8,128)(2,1)S(1)}, bf16[1,480,320]{1,2,0:T(8,128)(2,1)S(1)}, u32[]{:S(2)}, u32[]{:S(2)}) collective-permute-start(bf16[1,480,320]{1,2,0:T(8,128)(2,1)S(1)} %get-tuple-element.11), channel_id=1, source_target_pairs={{16,0},{32,16},{48,32},{64,48},{80,64},{96,80},{112,96},{128,112},... | collective-permute-start | bytes 921608 | tf_op jit(solution)/shard_map/ppermute | solution.py:19
  108.9 15.7 %collective-permute-start.2 = (bf16[1,480,320]{1,2,0:T(8,128)(2,1)S(1)}, bf16[1,480,320]{1,2,0:T(8,128)(2,1)S(1)}, u32[]{:S(2)}, u32[]{:S(2)}) collective-permute-start(bf16[1,480,320]{1,2,0:T(8,128)(2,1)S(1)} %get-tuple-element.12), channel_id=1, source_target_pairs={{0,16},{16,32},{32,48},{48,64},{64,80},{80,96},{96,112},{112,128},... | collective-permute-start | bytes 921608 | tf_op jit(solution)/shard_map/ppermute | solution.py:17
  139.7 3.2 copy-start.6
  164.4 4.1 %copy-start.14 = (f32[320]{0:T(512)S(1)}, f32[320]{0:T(512)}, u32[]{:S(2)}) copy-start(f32[320]{0:T(512)} %param.15) | copy-start | bytes 3844
  222.3 5.0 %copy-start.8 = (bf16[320,320]{1,0:T(8,128)(2,1)S(1)}, bf16[320,320]{1,0:T(8,128)(2,1)}, u32[]{:S(2)}) copy-start(bf16[320,320]{1,0:T(8,128)(2,1)} %param.17) | copy-start | bytes 614404
  223.7 7.0 %copy-start.9 = (bf16[320,320]{1,0:T(8,128)(2,1)S(1)}, bf16[320,320]{1,0:T(8,128)(2,1)}, u32[]{:S(2)}) copy-start(bf16[320,320]{1,0:T(8,128)(2,1)} %param.16) | copy-start | bytes 614404
  227.3 3.5 copy-start.3
  227.3 5.4 %copy-start.10 = (bf16[320,320]{1,0:T(8,128)(2,1)S(1)}, bf16[320,320]{1,0:T(8,128)(2,1)}, u32[]{:S(2)}) copy-start(bf16[320,320]{1,0:T(8,128)(2,1)} %param.18) | copy-start | bytes 614404
  312.1 1.7 copy-start.7
  321.2 46.4 %all-to-all-start.1 = ((bf16[64,1,30,320]{3,2,1,0:T(8,128)(2,1)}), bf16[64,1,30,320]{3,2,1,0:T(8,128)(2,1)}, u32[]{:S(2)}, u32[]{:S(2)}) async-start(bf16[64,1,30,320]{3,2,1,0:T(8,128)(2,1)} %copy.97), calls=%async_computation.1 | async-start | bytes 3145728 | tf_op jit(solution)/shard_map/all_to_all | solution.py:113
  369.7 5.6 %copy-start.2 = (f32[1920,320]{0,1:T(8,128)S(1)}, f32[1920,320]{0,1:T(8,128)}, u32[]{:S(2)}) copy-start(f32[1920,320]{0,1:T(8,128)} %convolution_add_fusion.1) | copy-start | bytes 7372804
  369.7 5.6 %copy-start.11 = (bf16[320,320]{1,0:T(8,128)(2,1)S(1)}, bf16[320,320]{1,0:T(8,128)(2,1)}, u32[]{:S(2)}) copy-start(bf16[320,320]{1,0:T(8,128)(2,1)} %param.19) | copy-start | bytes 614404
  379.8 10.9 %copy-start.1 = (bf16[3,3,320,320]{3,2,1,0:T(8,128)(2,1)S(1)}, bf16[3,3,320,320]{3,2,1,0:T(8,128)(2,1)}, u32[]{:S(2)}) copy-start(bf16[3,3,320,320]{3,2,1,0:T(8,128)(2,1)} %param.12) | copy-start | bytes 5529604
where the time goes:
time: 397 us; the launch traced here: 391 us
  local copies, waits for them, and re-layouts  195 us (49%)
  waiting for transfers between devices  62.7 us (16%)
  blocking collectives  48.7 us (12%)
  matrix products  34.7 us (9%)
  other arithmetic  26.2 us (7%)
  starting transfers between devices  23.4 us (6%)
    all_to_all x1, blocking collectives, local(): lax.all_to_all(normed.reshape(frames_here, groups, per_group, chans), 'fr...  48.7 us
    all_to_all x1, waiting for transfers between devices, local(): lax.all_to_all(attended, 'frame', split_axis=0, concat_axis=1, tiled=True)  31.6 us
    another operation x2, local copies, waits for them, and re-layouts, attend_heads(): k_split = keys.reshape(frames, pixels, heads, HEAD_DIM)  25.6 us
    another operation x2, local copies, waits for them, and re-layouts, attend_heads(): q_split = queries.reshape(frames, pixels, heads, HEAD_DIM)  25.3 us
    another operation x2, local copies, waits for them, and re-layouts, attend_heads(): v_split = values.reshape(frames, pixels, heads, HEAD_DIM)  22.7 us
    ppermute x2, waiting for transfers between devices, extended(): lax.ppermute(tail, axis, [(i, (i + 1) % count) for i in range(ends)])  16.5 us
    reshape x3, local copies, waits for them, and re-layouts, temporal_mix(): return total.reshape(frames, pixels, chans)  16.4 us
    ppermute x2, waiting for transfers between devices, extended(): lax.ppermute(head, axis, [((i + 1) % count, i) for i in range(ends)])  14.6 us
  transfers between devices with their start and end apart: 5, of which 5 were waited for; matrix products, arithmetic and copies ran while one was open for 4% of the time, Pallas kernels for 0%

commit v1 on v0

--- a/solution.py
+++ b/solution.py
@@ -110,7 +110,12 @@
     attended = attend_heads(
         project(moved, query_weight), project(moved, key_weight), project(moved, value_weight)
     ).reshape(frames_here * groups, 1, per_group, chans)
-    returned = lax.all_to_all(attended, "frame", split_axis=0, concat_axis=1, tiled=True)
+    returned = jnp.concatenate(
+        lax.all_to_all(
+            jnp.stack(jnp.split(attended, lax.axis_size("frame"), axis=0)), "frame", 0, 0
+        ),
+        axis=1,
+    )
     mixed = jnp.dot(returned.reshape(-1, chans), out_weight, preferred_element_type=jnp.float32)
     result = hidden_two.reshape(-1, chans) + mixed
     return result.reshape(frames_here, rows_here, width, chans)

time: 397 us -> 441 us (1.11)
  local copies, waits for them, and re-layouts: 195 us -> 242 us
    unnamed x33 -> x56, local copies, waits for them, and re-layouts: 4.05 us -> 25.6 us
    another operation x0 -> x18, local copies, waits for them, and re-layouts: none -> 17.4 us  [the longest x17 13.9 us: local(): jnp.stack(jnp.split(attended, lax.axis_size('frame'), axis=0))]
    split x0 -> x17, local copies, waits for them, and re-layouts: none -> 14.6 us  [local(): jnp.split(attended, lax.axis_size('frame'), axis=0)]
    convert_element_type x1 -> x0, local copies, waits for them, and re-layouts: 4.71 us -> none  [attend_heads(): return summed.reshape(frames, pixels, chans).astype(jnp.bfloat16)]
  transfers between devices with their start and end apart: 5 -> 5, of which waited for: 5 -> 5; matrix products, arithmetic and copies ran while one was open for 4% -> 3% of each run, Pallas kernels for 0% -> 0%
where the time goes in v1:
time: 441 us; the launch traced here: 435 us
  local copies, waits for them, and re-layouts  242 us (55%)
  waiting for transfers between devices  60.4 us (14%)
  blocking collectives  48.7 us (11%)
  matrix products  34.8 us (8%)
  other arithmetic  24.9 us (6%)
  starting transfers between devices  23.4 us (5%)
    all_to_all x1, blocking collectives, local(): lax.all_to_all(normed.reshape(frames_here, groups, per_group, chans), 'fr...  48.7 us
    all_to_all x1, waiting for transfers between devices, local(): lax.all_to_all(jnp.stack(jnp.split(attended, lax.axis_size('frame'), axis...  29.3 us
    unnamed x56, local copies, waits for them, and re-layouts  25.6 us
    another operation x2, local copies, waits for them, and re-layouts, attend_heads(): k_split = keys.reshape(frames, pixels, heads, HEAD_DIM)  25.6 us
    another operation x2, local copies, waits for them, and re-layouts, attend_heads(): v_split = values.reshape(frames, pixels, heads, HEAD_DIM)  25.4 us
    another operation x2, local copies, waits for them, and re-layouts, attend_heads(): q_split = queries.reshape(frames, pixels, heads, HEAD_DIM)  25.3 us
    ppermute x2, waiting for transfers between devices, extended(): lax.ppermute(tail, axis, [(i, (i + 1) % count) for i in range(ends)])  16.5 us
    reshape x3, local copies, waits for them, and re-layouts, temporal_mix(): return total.reshape(frames, pixels, chans)  16.4 us
  transfers between devices with their start and end apart: 5, of which 5 were waited for; matrix products, arithmetic and copies ran while one was open for 3% of the time, Pallas kernels for 0%

profile of v1, /device:TPU:63, one launch (start us, length us, event | category | flops | bytes accessed | tf_op | source)
XLA Modules:
  0.0 434.5 jit_solution(2943173376235627700)
XLA Ops:
  16.5 11.6 %collective-permute-done.1 = bf16[4,1,240,320]{2,3,1,0:T(8,128)(2,1)} collective-permute-done((bf16[4,1,240,320]{2,3,1,0:T(8,128)(2,1)}, bf16[4,1,240,320]{2,3,1,0:T(8,128)(2,1)}, u32[]{:S(2)}, u32[]{:S(2)}) %collective-permute-start.1) | collective-permute-done | bytes 614432 | tf_op jit(solution)/shard_map/ppermute | solution.py:19
  29.6 15.3 %collective-permute-done = bf16[4,1,240,320]{2,3,1,0:T(8,128)(2,1)} collective-permute-done((bf16[4,1,240,320]{2,3,1,0:T(8,128)(2,1)}, bf16[4,1,240,320]{2,3,1,0:T(8,128)(2,1)}, u32[]{:S(2)}, u32[]{:S(2)}) %collective-permute-start) | collective-permute-done | bytes 614432 | tf_op jit(solution)/shard_map/ppermute | solution.py:17
  52.2 5.8 %reshape.172 = bf16[4,4,8,31,320]{4,3,2,1,0:T(8,128)(2,1)} reshape(bf16[4,4,248,320]{3,2,1,0:T(8,128)(2,1)} %pad) | data formatting | bytes 5079040 | tf_op jit(solution)/shard_map/conv_general_dilated | solution.py:84
  61.6 6.6 %fusion.25 = f32[2,32,31,320]{3,1,2,0:T(8,128)S(1)} fusion(bf16[3,3,320,320]{3,2,1,0:T(8,128)(2,1)S(1)} %copy-done, bf16[4,4,8,33,320]{4,3,2,1,0:T(8,128)(2,1)S(1)} %fusion.4, pred[32,31]{0,1:T(8,128)(4,1)S(1)} %copy-done.19), kind=kOutput, calls=%fused_computation.42 | convolution fusion | flops 3657543680 | bytes 7087072 | tf_op jit(solution)/shard_map/conv_general_dilated | solution.py:84
  86.9 4.9 %copy.111 = bf16[4,2,240,320]{2,1,0,3:T(2,128)(2,1)} copy(bf16[4,2,240,320]{3,2,0,1:T(8,128)(2,1)} %multiply_convert_fusion) | data formatting | bytes 2457600 | tf_op jit(solution)/shard_map/convert_element_type | solution.py:95
  91.8 4.9 %convert_element_type.39 = bf16[1920,320]{0,1:T(8,128)(2,1)} reshape(bf16[4,2,240,320]{2,1,0,3:T(2,128)(2,1)} %copy.111) | data formatting | bytes 2457600 | tf_op jit(solution)/shard_map/convert_element_type | solution.py:95
  96.7 4.8 %reshape.162 = f32[4,480,320]{1,2,0:T(8,128)} reshape(f32[4,2,240,320]{2,1,3,0:T(2,128)} %copy.108) | data formatting | bytes 4915200 | tf_op jit(solution)/shard_map/reshape | solution.py:94
  107.8 8.1 %collective-permute-start.2 = (bf16[1,480,320]{1,2,0:T(8,128)(2,1)S(1)}, bf16[1,480,320]{1,2,0:T(8,128)(2,1)S(1)}, u32[]{:S(2)}, u32[]{:S(2)}) collective-permute-start(bf16[1,480,320]{1,2,0:T(8,128)(2,1)S(1)} %get-tuple-element.28), channel_id=1, source_target_pairs={{0,16},{16,32},{32,48},{48,64},{64,80},{80,96},{96,112},{112,128},... | collective-permute-start | bytes 921608 | tf_op jit(solution)/shard_map/ppermute | solution.py:17
  126.8 4.4 %reshape.164 = bf16[1920,320]{0,1:T(8,128)(2,1)} reshape(bf16[4,480,320]{1,0,2:T(4,128)(2,1)} %copy.112) | data formatting | bytes 2457600 | tf_op jit(solution)/shard_map/reshape | solution.py:61
  145.1 6.7 %reshape.167 = f32[4,2,240,320]{2,1,0,3:T(2,128)} reshape(f32[1920,320]{0,1:T(8,128)} %convolution_add_fusion.1) | data formatting | bytes 4915200 | tf_op jit(solution)/shard_map/reshape | solution.py:65
  155.2 5.6 %copy.116 = f32[4,2,240,320]{3,2,0,1:T(8,128)} copy(f32[4,2,240,320]{2,1,0,3:T(2,128)} %reshape.167) | data formatting | bytes 4915200 | tf_op jit(solution)/shard_map/reshape | solution.py:65
  167.5 5.0 %fusion.18 = bf16[4,16,30,320]{3,0,2,1:T(4,128)(2,1)S(1)} fusion(f32[4,16,30,320]{3,0,2,1:T(4,128)} %bitcast.104, f32[4,16,30,320]{3,2,1,0:T(8,128)} %reshape.166, f32[320]{0:T(512)S(1)} %copy-done.18, f32[4,16,30]{0,2,1:T(8,128)S(1)} %copy.118), kind=kLoop, calls=%fused_computation.28 | loop fusion | flops 2457600 | bytes 6152960 | tf_op jit(solution)/shard_map/convert_element_type | solution.py:99
  172.5 48.7 %all_to_all.20 = bf16[4,16,30,320]{3,0,2,1:T(4,128)(2,1)S(1)} all-to-all(bf16[4,16,30,320]{3,0,2,1:T(4,128)(2,1)S(1)} %fusion.18), channel_id=1, replica_groups=mesh['frame'=16,'row'=16] {'frame'}, dimensions={1} | all-to-all | bytes 2457600 | tf_op jit(solution)/shard_map/all_to_all | solution.py:102
  233.5 15.4 %reshape.180 = bf16[64,30,5,64]{1,0,3,2:T(8,128)(2,1)} reshape(bf16[1920,320]{0,1:T(8,128)(2,1)} %convolution_convert_fusion.2) | data formatting | bytes 2457600 | tf_op jit(solution)/shard_map/reshape;reshape | solution.py:42
  248.9 10.0 %copy.125 = bf16[64,30,5,64]{3,0,2,1:T(8,128)(2,1)} copy(bf16[64,30,5,64]{1,0,3,2:T(8,128)(2,1)} %reshape.180) | data formatting | bytes 2457600 | tf_op jit(solution)/shard_map/reshape;reshape | solution.py:42
  258.9 15.4 %reshape.181 = bf16[64,30,5,64]{1,0,3,2:T(8,128)(2,1)} reshape(bf16[1920,320]{0,1:T(8,128)(2,1)} %convolution_convert_fusion.1) | data formatting | bytes 2457600 | tf_op jit(solution)/shard_map/reshape;reshape | solution.py:40
  274.3 9.9 %copy.123 = bf16[64,30,5,64]{3,0,2,1:T(8,128)(2,1)} copy(bf16[64,30,5,64]{1,0,3,2:T(8,128)(2,1)} %reshape.181) | data formatting | bytes 2457600 | tf_op jit(solution)/shard_map/reshape;reshape | solution.py:40
  284.3 15.6 %reshape.182 = bf16[64,30,5,64]{1,0,3,2:T(8,128)(2,1)} reshape(bf16[1920,320]{0,1:T(8,128)(2,1)} %convolution_convert_fusion) | data formatting | bytes 2457600 | tf_op jit(solution)/shard_map/reshape;reshape | solution.py:41
  299.9 10.0 %copy.124 = bf16[64,30,5,64]{3,0,2,1:T(8,128)(2,1)} copy(bf16[64,30,5,64]{1,0,3,2:T(8,128)(2,1)} %reshape.182) | data formatting | bytes 2457600 | tf_op jit(solution)/shard_map/reshape;reshape | solution.py:41
  368.4 6.4 %all-to-all-start.1 = ((bf16[16,4,1,30,320]{4,1,3,2,0:T(4,128)(2,1)}), bf16[16,4,1,30,320]{4,1,3,2,0:T(4,128)(2,1)}, u32[]{:S(2)}, u32[]{:S(2)}) async-start(bf16[16,4,1,30,320]{4,1,3,2,0:T(4,128)(2,1)} %constant_dynamic-update-slice_fusion), calls=%async_computation.1 | async-start | bytes 2949120 | tf_op jit(solution)/shard_map/all_to_all | solution.py:114
  378.1 5.0 %reshape.161 = f32[1920,320]{0,1:T(8,128)} reshape(f32[4,2,240,320]{2,1,0,3:T(2,128)} %copy.107) | data formatting | bytes 4915200 | tf_op jit(solution)/shard_map/reshape | solution.py:94
  383.1 29.3 %all-to-all-done.1 = bf16[16,4,1,30,320]{4,1,3,2,0:T(4,128)(2,1)} async-done(((bf16[16,4,1,30,320]{4,1,3,2,0:T(4,128)(2,1)}), bf16[16,4,1,30,320]{4,1,3,2,0:T(4,128)(2,1)}, u32[]{:S(2)}, u32[]{:S(2)}) %all-to-all-start.1) | async-done | bytes 1228832 | tf_op jit(solution)/shard_map/all_to_all | solution.py:114
  418.8 4.5 %convolution_add_fusion = f32[1920,320]{0,1:T(8,128)} fusion(bf16[1920,320]{1,0:T(8,128)(2,1)} %reshape_reshape.21, bf16[320,320]{1,0:T(8,128)(2,1)S(1)} %copy-done.15, f32[1920,320]{0,1:T(8,128)} %reshape.161, f32[1920,320]{0,1:T(8,128)S(1)} %copy-done.2), kind=kOutput, calls=%fused_computation.32 | convolution fusion | flops 394444800 | bytes 8806400 | tf_op jit(solution)/shard_map/dot_general | solution.py:119
  423.3 6.9 %reshape.169 = f32[4,2,240,320]{2,1,0,3:T(2,128)} reshape(f32[1920,320]{0,1:T(8,128)} %convolution_add_fusion) | data formatting | bytes 4915200 | tf_op jit(solution)/shard_map/reshape | solution.py:121
  (144 shorter events, 173.0 us)
Async XLA Ops:
  0.0 61.6 %copy-start = (bf16[3,3,320,320]{3,2,1,0:T(8,128)(2,1)S(1)}, bf16[3,3,320,320]{3,2,1,0:T(8,128)(2,1)}, u32[]{:S(2)}) copy-start(bf16[3,3,320,320]{3,2,1,0:T(8,128)(2,1)} %param.12) | copy-start | bytes 5529604
  0.0 4.6 %copy-start.17 = (f32[320]{0:T(512)S(1)}, f32[320]{0:T(512)}, u32[]{:S(2)}) copy-start(f32[320]{0:T(512)} %param.11) | copy-start | bytes 3844
  2.7 1.9 copy-start.3
  9.9 18.2 %collective-permute-start.1 = (bf16[4,1,240,320]{2,3,1,0:T(8,128)(2,1)}, bf16[4,1,240,320]{2,3,1,0:T(8,128)(2,1)}, u32[]{:S(2)}, u32[]{:S(2)}) collective-permute-start(bf16[4,1,240,320]{2,3,1,0:T(8,128)(2,1)} %copy.102), channel_id=1, source_target_pairs={{1,0},{2,1},{3,2},{4,3},{5,4},{6,5},{7,6},{8,7},{9,8},{10,9},{11,1... | collective-permute-start | bytes 1843208 | tf_op jit(solution)/shard_map/ppermute | solution.py:19
  13.0 31.9 %collective-permute-start = (bf16[4,1,240,320]{2,3,1,0:T(8,128)(2,1)}, bf16[4,1,240,320]{2,3,1,0:T(8,128)(2,1)}, u32[]{:S(2)}, u32[]{:S(2)}) collective-permute-start(bf16[4,1,240,320]{2,3,1,0:T(8,128)(2,1)} %copy.101), channel_id=1, source_target_pairs={{0,1},{1,2},{2,3},{3,4},{4,5},{5,6},{6,7},{7,8},{8,9},{9,10},{10,1... | collective-permute-start | bytes 1843208 | tf_op jit(solution)/shard_map/ppermute | solution.py:17
  59.2 2.4 copy-start.19
  82.0 2.9 copy-start.16
  101.5 14.4 %copy-start.6 = (bf16[1920,320]{0,1:T(8,128)(2,1)S(1)}, bf16[1920,320]{0,1:T(8,128)(2,1)}, u32[]{:S(2)}) copy-start(bf16[1920,320]{0,1:T(8,128)(2,1)} %convert_element_type.39) | copy-start | bytes 3686404
  104.3 17.9 %collective-permute-start.3 = (bf16[1,480,320]{1,2,0:T(8,128)(2,1)S(1)}, bf16[1,480,320]{1,2,0:T(8,128)(2,1)S(1)}, u32[]{:S(2)}, u32[]{:S(2)}) collective-permute-start(bf16[1,480,320]{1,2,0:T(8,128)(2,1)S(1)} %get-tuple-element.27), channel_id=1, source_target_pairs={{16,0},{32,16},{48,32},{64,48},{80,64},{96,80},{112,96},{128,112},... | collective-permute-start | bytes 921608 | tf_op jit(solution)/shard_map/ppermute | solution.py:19
  107.8 15.7 %collective-permute-start.2 = (bf16[1,480,320]{1,2,0:T(8,128)(2,1)S(1)}, bf16[1,480,320]{1,2,0:T(8,128)(2,1)S(1)}, u32[]{:S(2)}, u32[]{:S(2)}) collective-permute-start(bf16[1,480,320]{1,2,0:T(8,128)(2,1)S(1)} %get-tuple-element.28), channel_id=1, source_target_pairs={{0,16},{16,32},{32,48},{48,64},{64,80},{80,96},{96,112},{112,128},... | collective-permute-start | bytes 921608 | tf_op jit(solution)/shard_map/ppermute | solution.py:17
  138.6 3.2 copy-start.7
  163.3 4.1 copy-start.18
  221.2 5.0 %copy-start.12 = (bf16[320,320]{1,0:T(8,128)(2,1)S(1)}, bf16[320,320]{1,0:T(8,128)(2,1)}, u32[]{:S(2)}) copy-start(bf16[320,320]{1,0:T(8,128)(2,1)} %param.17) | copy-start | bytes 614404
  222.7 7.0 %copy-start.13 = (bf16[320,320]{1,0:T(8,128)(2,1)S(1)}, bf16[320,320]{1,0:T(8,128)(2,1)}, u32[]{:S(2)}) copy-start(bf16[320,320]{1,0:T(8,128)(2,1)} %param.16) | copy-start | bytes 614404
  226.2 3.4 copy-start.4
  226.2 5.4 %copy-start.14 = (bf16[320,320]{1,0:T(8,128)(2,1)S(1)}, bf16[320,320]{1,0:T(8,128)(2,1)}, u32[]{:S(2)}) copy-start(bf16[320,320]{1,0:T(8,128)(2,1)} %param.18) | copy-start | bytes 614404
  313.7 1.7 copy-start.8
  344.4 22.6 %copy-start.10 = (bf16[1,4,1,30,320]{4,1,3,2,0:T(4,128)(2,1)S(1)}, bf16[1,4,1,30,320]{4,1,3,2,0:T(4,128)(2,1)}, u32[]{:S(2)}) copy-start(bf16[1,4,1,30,320]{4,1,3,2,0:T(4,128)(2,1)} %stack.65) | copy-start | bytes 230404
  344.4 23.3 %copy-start.9 = (bf16[1,4,1,30,320]{4,1,3,2,0:T(4,128)(2,1)S(1)}, bf16[1,4,1,30,320]{4,1,3,2,0:T(4,128)(2,1)}, u32[]{:S(2)}) copy-start(bf16[1,4,1,30,320]{4,1,3,2,0:T(4,128)(2,1)} %stack.66) | copy-start | bytes 230404
  345.3 21.1 %copy-start.11 = (bf16[1,4,1,30,320]{4,1,3,2,0:T(4,128)(2,1)S(1)}, bf16[1,4,1,30,320]{4,1,3,2,0:T(4,128)(2,1)}, u32[]{:S(2)}) copy-start(bf16[1,4,1,30,320]{4,1,3,2,0:T(4,128)(2,1)} %stack.64) | copy-start | bytes 230404
  368.4 44.0 %all-to-all-start.1 = ((bf16[16,4,1,30,320]{4,1,3,2,0:T(4,128)(2,1)}), bf16[16,4,1,30,320]{4,1,3,2,0:T(4,128)(2,1)}, u32[]{:S(2)}, u32[]{:S(2)}) async-start(bf16[16,4,1,30,320]{4,1,3,2,0:T(4,128)(2,1)} %constant_dynamic-update-slice_fusion), calls=%async_computation.1 | async-start | bytes 2949120 | tf_op jit(solution)/shard_map/all_to_all | solution.py:114
  412.4 6.4 %copy-start.2 = (f32[1920,320]{0,1:T(8,128)S(1)}, f32[1920,320]{0,1:T(8,128)}, u32[]{:S(2)}) copy-start(f32[1920,320]{0,1:T(8,128)} %convolution_add_fusion.1) | copy-start | bytes 7372804
  412.4 6.4 %copy-start.15 = (bf16[320,320]{1,0:T(8,128)(2,1)S(1)}, bf16[320,320]{1,0:T(8,128)(2,1)}, u32[]{:S(2)}) copy-start(bf16[320,320]{1,0:T(8,128)(2,1)} %param.19) | copy-start | bytes 614404
  423.3 10.9 %copy-start.1 = (bf16[3,3,320,320]{3,2,1,0:T(8,128)(2,1)S(1)}, bf16[3,3,320,320]{3,2,1,0:T(8,128)(2,1)}, u32[]{:S(2)}) copy-start(bf16[3,3,320,320]{3,2,1,0:T(8,128)(2,1)} %param.12) | copy-start | bytes 5529604
  (1 other events, 1.1 us)
